TPU v7x, 256 devices: a whole 4x4x8 slice. The times are simulated.
256 devices in a mesh: grp: 8 (over z), feat: 32 (over x, y, core).
Axes of the slice: x: 4, y: 4, z: 8, core: 2. Of those that a mesh axis runs over, the one named last changes fastest.
Arguments:
- features: bfloat16 [65536, 512], P(('grp', 'feat')), may hold values from -6 to 6
- adj_tiles: bfloat16 [512, 16, 128, 128], P(('grp', 'feat')), may hold values from 0.0099487305 to 1
- src_block: int32 [512, 16], P(('grp', 'feat')), may hold values from 0 to 63, as said below
- counts: int32 [512], P(('grp', 'feat')), may hold values from 1 to 16, as said below
- w_self: bfloat16 [512, 512], replicated, may hold values from -0.25 to 0.25
- w_neigh: bfloat16 [512, 512], replicated, may hold values from -0.25 to 0.25
- multiplier: float32 [512], replicated, may hold values from 0.5 to 2
- bit_shift: int32 [512], replicated, may hold values from 0 to 2
- cotangent: bfloat16 [65536, 512], P(('grp', 'feat')), may hold values from -6 to 6
Outputs:
- output: bfloat16 [65536, 512], P(('grp', 'feat'))
- grad_features: bfloat16 [65536, 512], P(('grp', 'feat'))
- grad_self: float32 [512, 512], replicated
- grad_neigh: float32 [512, 512], replicated
Inputs may be any that keep to these rules, and one draw needn't show every extreme that they name: src_block[i, k] is a block of block i's own group, held by a device at most 2 positions from block i's device in the group's cyclic order of devices (block i is held by device (i % 64) // 2 of its group, which holds 2 consecutive blocks); the distance 2 is reached in both directions in every draw. Slots k >= counts[i] take no part.
All inputs are finite; a program needn't handle non-finite values.
Results may differ from a plain program's by a relative error of at most 0.0059.
Values may be sent and summed in bfloat16 or wider, within the bound.
No kernel may reach another device: no remote copies, remote signals or barrier semaphores. Data moves between devices by JAX's collectives and lax.ppermute only.
A program may use at most 64 MiB of HBM per device.

v0:
```python
import math
import jax
import jax.numpy as jnp
from jax import lax
from jax.sharding import PartitionSpec as P

SPAN = 2


def passed_along(x, axis, by):
    peers = lax.axis_size(axis)
    return lax.ppermute(x, axis, [(i, (i + by) % peers) for i in range(peers)])


def fetch_near(shard_piece, steps_by):
    return passed_along(shard_piece, "feat", steps_by)


def return_near(shard_piece, steps_by):
    return passed_along(shard_piece, "feat", steps_by)


def local(
    features, adj_tiles, src_block, counts, w_self, w_neigh, multiplier, bit_shift, cotangent
):
    num_blocks = adj_tiles.shape[0]
    num_slots = adj_tiles.shape[1]
    block_len = adj_tiles.shape[2]
    feature_width = features.shape[1]
    row_count = features.shape[0]
    feat_count = lax.axis_size("feat")
    my_index = lax.axis_index("feat")
    live_mask = jnp.arange(num_slots, dtype=jnp.int32)[None, :] < counts[:, None]
    masked = jnp.where(live_mask[:, :, None, None], adj_tiles, jnp.zeros_like(adj_tiles))
    degree = jnp.sum(masked, axis=(1, 3), dtype=jnp.float32)
    inv_root = lax.rsqrt(degree)
    node_blocks = features.reshape(num_blocks, block_len, feature_width)
    pieces = {0: node_blocks}
    for offset in range(-SPAN, SPAN + 1):
        if offset != 0:
            pieces[offset] = fetch_near(node_blocks, -offset)
    source_pool = jnp.concatenate([pieces[offset] for offset in range(-SPAN, SPAN + 1)], axis=0)
    relative = (src_block // num_blocks - my_index + SPAN) % feat_count
    slot_index = relative * num_blocks + src_block % num_blocks
    flat_index = slot_index.reshape(-1)
    sources = jnp.take(source_pool, flat_index, axis=0).reshape(
        num_blocks, num_slots, block_len, feature_width
    )
    summed = jnp.einsum("bkij,bkjf->bif", masked, sources, preferred_element_type=jnp.float32)
    aggregated = (
        (summed * inv_root[:, :, None]).astype(jnp.bfloat16).reshape(row_count, feature_width)
    )
    preact = jnp.dot(features, w_self, preferred_element_type=jnp.float32)
    preact = preact + jnp.dot(aggregated, w_neigh, preferred_element_type=jnp.float32)
    scale = multiplier * jnp.exp2(-bit_shift.astype(jnp.float32))
    scaled = preact * scale
    sigmoid_val = jax.nn.sigmoid(scaled)
    output = (scaled * sigmoid_val).astype(jnp.bfloat16)
    grad_pre = (
        cotangent.astype(jnp.float32) * sigmoid_val * (1.0 + scaled * (1.0 - sigmoid_val)) * scale
    ).astype(jnp.bfloat16)
    part_self = jnp.dot(features.T, grad_pre, preferred_element_type=jnp.float32)
    part_neigh = jnp.dot(aggregated.T, grad_pre, preferred_element_type=jnp.float32)
    total_self, total_neigh = lax.psum((part_self, part_neigh), ("grp", "feat"))
    grad_scale = 1.0 / math.sqrt(row_count * lax.axis_size("grp") * feat_count)
    own_part = jnp.dot(grad_pre, w_self.T, preferred_element_type=jnp.float32)
    back = jnp.dot(grad_pre, w_neigh.T, preferred_element_type=jnp.float32).reshape(
        num_blocks, block_len, feature_width
    )
    back = (back * inv_root[:, :, None]).astype(jnp.bfloat16)
    contrib = jnp.einsum("bkij,bif->bkjf", masked, back, preferred_element_type=jnp.float32)
    contrib_flat = contrib.reshape(num_blocks * num_slots, block_len * feature_width)
    window_count = (2 * SPAN + 1) * num_blocks
    grouped = jax.ops.segment_sum(contrib_flat, flat_index, num_segments=window_count)
    window = lax.optimization_barrier(grouped.astype(jnp.bfloat16))
    window = window.reshape(window_count, block_len, feature_width)

    def window_piece(offset):
        first_block = (offset + SPAN) * num_blocks
        return window[first_block : first_block + num_blocks]

    spread_blocks = window_piece(0).astype(jnp.float32)
    for offset in range(-SPAN, SPAN + 1):
        if offset != 0:
            arrived = return_near(window_piece(offset), offset)
            spread_blocks = spread_blocks + arrived.astype(jnp.float32)
    spread = spread_blocks.reshape(row_count, feature_width)
    grad_features = (own_part + spread).astype(jnp.bfloat16)
    return (output, grad_features, total_self * grad_scale, total_neigh * grad_scale)


def solution(mesh):
    return jax.shard_map(
        local,
        mesh=mesh,
        in_specs=(
            P(("grp", "feat"), None),
            P(("grp", "feat"), None, None, None),
            P(("grp", "feat"), None),
            P(("grp", "feat")),
            P(),
            P(),
            P(),
            P(),
            P(("grp", "feat"), None),
        ),
        out_specs=(P(("grp", "feat"), None), P(("grp", "feat"), None), P(), P()),
        check_vma=False,
    )
```

profile of v0, /device:TPU:2, one launch (start us, length us, event | category | flops | bytes accessed | tf_op | source)
XLA Modules:
  0.0 402.8 jit_solution(4255000697265647718)
XLA Ops:
  7.2 1.7 collective-permute-start
  8.9 3.9 collective-permute-start.2
  14.7 2.2 fusion.33
  17.6 1.6 convert_reduce_fusion
  20.6 1.4 collective-permute-done.3
  22.0 2.8 gather_fusion
  24.8 3.1 fusion.11
  27.9 1.2 multiply_convert_fusion.1
  29.2 1.3 fusion.35
  30.5 1.3 convolution_bitcast_fusion
  32.1 1.4 fusion.14
  33.5 8.1 %copy.21 = f32[4,8,128,512]{3,1,2,0:T(8,128)} copy(f32[4,8,128,512]{3,2,1,0:T(8,128)S(1)} %bitcast.65) | data formatting | bytes 16777216
  41.6 2.2 broadcast_in_dim.35
  43.9 75.4 %scatter_fusion = f32[10,65536]{1,0:T(8,128)} fusion(f32[10,65536]{1,0:T(8,128)} %broadcast_in_dim.35, s32[32]{0:T(128)S(1)} %reshape.113, f32[32,65536]{1,0:T(8,128)} %bitcast.64), kind=kCustom, calls=%fused_computation.1 | custom fusion | flops 2097152 | bytes 25165952 | tf_op jit(solution)/shard_map/scatter-add | solution.py:74
  119.3 2.4 convert_element_type.52
  122.6 4.9 %collective-permute-start.4 = (bf16[2,128,512]{2,1,0:T(8,128)(2,1)S(1)}, bf16[2,128,512]{2,1,0:T(8,128)(2,1)S(1)}, u32[]{:S(2)}, u32[]{:S(2)}) collective-permute-start(bf16[2,128,512]{2,1,0:T(8,128)(2,1)S(1)} %bitcast.78), channel_id=1, source_target_pairs={{0,30},{1,31},{2,0},{3,1},{4,2},{5,3},{6,4},{7,5},{8,6},{9,7},{10,... | collective-permute-start | bytes 786440 | tf_op jit(solution)/shard_map/ppermute | solution.py:12
  128.3 3.0 collective-permute-done.4
  131.4 2.8 collective-permute-done.5
  134.2 3.1 collective-permute-done.6
  137.2 2.4 collective-permute-done.7
  140.8 250.7 %all-reduce.3.cloned.1.call-done = (f32[512,512]{0,1:T(8,128)}, f32[512,512]{0,1:T(8,128)}) async-done(((f32[512,512]{0,1:T(8,128)}, f32[512,512]{0,1:T(8,128)}), (f32[512,512]{0,1:T(8,128)}, f32[512,512]{0,1:T(8,128)})) %all-reduce.3.cloned.1.call-update) | async-done | bytes 2097168 | tf_op jit(solution)/shard_map/psum | solution.py:64
  391.5 1.8 broadcast_multiply_fusion
  393.4 1.3 copy.15
  394.7 1.3 copy.16
  (43 shorter events, 7.3 us)
Async XLA Ops:
  7.2 20.8 %copy-start = (bf16[512,512]{1,0:T(8,128)(2,1)S(1)}, bf16[512,512]{1,0:T(8,128)(2,1)}, u32[]{:S(2)}) copy-start(bf16[512,512]{1,0:T(8,128)(2,1)} %param.14) | copy-start | bytes 1572868
  7.2 13.3 %copy-start.2 = (bf16[256,512]{1,0:T(8,128)(2,1)S(1)}, bf16[256,512]{1,0:T(8,128)(2,1)}, u32[]{:S(2)}) copy-start(bf16[256,512]{1,0:T(8,128)(2,1)} %param.9) | copy-start | bytes 786436
  7.2 384.4 %all-reduce.3.cloned.1.call-start = ((), (), s32[]{:S(2)}) async-start(), calls=%async_computation | async-start | bytes 4194304 | tf_op jit(solution)/shard_map/psum | solution.py:64
  7.2 12.1 %collective-permute-start = (bf16[2,128,512]{2,1,0:T(8,128)(2,1)}, bf16[2,128,512]{2,1,0:T(8,128)(2,1)S(1)}, u32[]{:S(2)}, u32[]{:S(2)}) collective-permute-start(bf16[2,128,512]{2,1,0:T(8,128)(2,1)} %bitcast.67), channel_id=1, source_target_pairs={{0,2},{1,3},{2,4},{3,5},{4,6},{5,7},{6,8},{7,9},{8,10},{9,11},{10,... | collective-permute-start | bytes 786440 | tf_op jit(solution)/shard_map/ppermute | solution.py:12
  8.9 11.6 %collective-permute-start.1 = (bf16[2,128,512]{2,1,0:T(8,128)(2,1)}, bf16[2,128,512]{2,1,0:T(8,128)(2,1)S(1)}, u32[]{:S(2)}, u32[]{:S(2)}) collective-permute-start(bf16[2,128,512]{2,1,0:T(8,128)(2,1)} %bitcast.68), channel_id=1, source_target_pairs={{0,1},{1,2},{2,3},{3,4},{4,5},{5,6},{6,7},{7,8},{8,9},{9,10},{10,1... | collective-permute-start | bytes 786440 | tf_op jit(solution)/shard_map/ppermute | solution.py:12
  8.9 11.7 %collective-permute-start.2 = (bf16[2,128,512]{2,1,0:T(8,128)(2,1)}, bf16[2,128,512]{2,1,0:T(8,128)(2,1)S(1)}, u32[]{:S(2)}, u32[]{:S(2)}) collective-permute-start(bf16[2,128,512]{2,1,0:T(8,128)(2,1)} %bitcast.69), channel_id=1, source_target_pairs={{0,31},{1,0},{2,1},{3,2},{4,3},{5,4},{6,5},{7,6},{8,7},{9,8},{10,9... | collective-permute-start | bytes 786440 | tf_op jit(solution)/shard_map/ppermute | solution.py:12
  12.7 9.3 %collective-permute-start.3 = (bf16[2,128,512]{2,1,0:T(8,128)(2,1)}, bf16[2,128,512]{2,1,0:T(8,128)(2,1)S(1)}, u32[]{:S(2)}, u32[]{:S(2)}) collective-permute-start(bf16[2,128,512]{2,1,0:T(8,128)(2,1)} %bitcast.70), channel_id=1, source_target_pairs={{0,30},{1,31},{2,0},{3,1},{4,2},{5,3},{6,4},{7,5},{8,6},{9,7},{10,... | collective-permute-start | bytes 786440 | tf_op jit(solution)/shard_map/ppermute | solution.py:12
  22.0 2.8 copy-start.1
  24.8 3.1 copy-start.4
  24.8 3.1 copy-start.5
  122.5 17.3 %copy-start.3 = (bf16[512,512]{1,0:T(8,128)(2,1)S(1)}, bf16[512,512]{1,0:T(8,128)(2,1)}, u32[]{:S(2)}) copy-start(bf16[512,512]{1,0:T(8,128)(2,1)} %param.13) | copy-start | bytes 1572868
  122.6 8.8 %collective-permute-start.4 = (bf16[2,128,512]{2,1,0:T(8,128)(2,1)S(1)}, bf16[2,128,512]{2,1,0:T(8,128)(2,1)S(1)}, u32[]{:S(2)}, u32[]{:S(2)}) collective-permute-start(bf16[2,128,512]{2,1,0:T(8,128)(2,1)S(1)} %bitcast.78), channel_id=1, source_target_pairs={{0,30},{1,31},{2,0},{3,1},{4,2},{5,3},{6,4},{7,5},{8,6},{9,7},{10,... | collective-permute-start | bytes 786440 | tf_op jit(solution)/shard_map/ppermute | solution.py:12
  127.5 6.7 %collective-permute-start.5 = (bf16[2,128,512]{2,1,0:T(8,128)(2,1)S(1)}, bf16[2,128,512]{2,1,0:T(8,128)(2,1)S(1)}, u32[]{:S(2)}, u32[]{:S(2)}) collective-permute-start(bf16[2,128,512]{2,1,0:T(8,128)(2,1)S(1)} %bitcast.79), channel_id=1, source_target_pairs={{0,31},{1,0},{2,1},{3,2},{4,3},{5,4},{6,5},{7,6},{8,7},{9,8},{10,9... | collective-permute-start | bytes 786440 | tf_op jit(solution)/shard_map/ppermute | solution.py:12
  127.6 9.6 %collective-permute-start.6 = (bf16[2,128,512]{2,1,0:T(8,128)(2,1)S(1)}, bf16[2,128,512]{2,1,0:T(8,128)(2,1)S(1)}, u32[]{:S(2)}, u32[]{:S(2)}) collective-permute-start(bf16[2,128,512]{2,1,0:T(8,128)(2,1)S(1)} %bitcast.80), channel_id=1, source_target_pairs={{0,1},{1,2},{2,3},{3,4},{4,5},{5,6},{6,7},{7,8},{8,9},{9,10},{10,1... | collective-permute-start | bytes 786440 | tf_op jit(solution)/shard_map/ppermute | solution.py:12
  128.2 11.4 %collective-permute-start.7 = (bf16[2,128,512]{2,1,0:T(8,128)(2,1)S(1)}, bf16[2,128,512]{2,1,0:T(8,128)(2,1)S(1)}, u32[]{:S(2)}, u32[]{:S(2)}) collective-permute-start(bf16[2,128,512]{2,1,0:T(8,128)(2,1)S(1)} %bitcast.81), channel_id=1, source_target_pairs={{0,2},{1,3},{2,4},{3,5},{4,6},{5,7},{6,8},{7,9},{8,10},{9,11},{10,... | collective-permute-start | bytes 786440 | tf_op jit(solution)/shard_map/ppermute | solution.py:12
Sparse Core Ops, SparseCore 0:
  121.8 269.6 all-reduce.2
where the time goes:
time: 403 us
  waiting for transfers between devices  265 us (66%)
  other arithmetic  84.4 us (21%)
  local copies, waits for them, and re-layouts  16.1 us (4%)
  between operations  14.2 us (4%)
  matrix products  11.9 us (3%)
  starting transfers between devices  11.6 us (3%)
    psum x1, waiting for transfers between devices, local(): total_self, total_neigh = lax.psum((part_self, part_neigh), ('grp', 'feat'))  251 us
    scatter-add x1, other arithmetic, local(): jax.ops.segment_sum(contrib_flat, flat_index, num_segments=window_count)  75.4 us
    ppermute x8, waiting for transfers between devices, passed_along(): return lax.ppermute(x, axis, [(i, (i + by) % peers) for i in range(peers)])  13.8 us
    ppermute x8, starting transfers between devices, passed_along(): return lax.ppermute(x, axis, [(i, (i + by) % peers) for i in range(peers)])  11.6 us
    unnamed x23, local copies, waits for them, and re-layouts  10.9 us
  transfers between devices with their start and end apart: 9, of which 7 were waited for; matrix products, arithmetic and copies ran while one was open for 2% of the time, Pallas kernels for 0%

commit v1 on v0

--- a/solution.py
+++ b/solution.py
@@ -61,7 +61,7 @@
     ).astype(jnp.bfloat16)
     part_self = jnp.dot(features.T, grad_pre, preferred_element_type=jnp.float32)
     part_neigh = jnp.dot(aggregated.T, grad_pre, preferred_element_type=jnp.float32)
-    total_self, total_neigh = lax.psum((part_self, part_neigh), ("grp", "feat"))
+    total_self, total_neigh = lax.psum(lax.psum((part_self, part_neigh), "feat"), "grp")
     grad_scale = 1.0 / math.sqrt(row_count * lax.axis_size("grp") * feat_count)
     own_part = jnp.dot(grad_pre, w_self.T, preferred_element_type=jnp.float32)
     back = jnp.dot(grad_pre, w_neigh.T, preferred_element_type=jnp.float32).reshape(

time: 403 us -> 250 us (0.62)
  waiting for transfers between devices: 265 us -> 112 us
    psum x1 -> x2, waiting for transfers between devices: 251 us -> 98.1 us  [the longest x1 67.2 us: local(): lax.psum(lax.psum((part_self, part_neigh), 'feat'), 'grp')]
  transfers between devices with their start and end apart: 9 -> 10, of which waited for: 7 -> 8; matrix products, arithmetic and copies ran while one was open for 2% -> 40% of each run, Pallas kernels for 0% -> 0%
where the time goes in v1:
time: 250 us
  waiting for transfers between devices  112 us (45%)
  other arithmetic  84.8 us (34%)
  local copies, waits for them, and re-layouts  16.1 us (6%)
  between operations  14.3 us (6%)
  matrix products  11.9 us (5%)
  starting transfers between devices  10.6 us (4%)
    scatter-add x1, other arithmetic, local(): jax.ops.segment_sum(contrib_flat, flat_index, num_segments=window_count)  75.9 us
    psum x1, waiting for transfers between devices, local(): lax.psum(lax.psum((part_self, part_neigh), 'feat'), 'grp')  67.2 us
    psum x1, waiting for transfers between devices, local(): lax.psum((part_self, part_neigh), 'feat')  30.9 us
    ppermute x8, waiting for transfers between devices, passed_along(): return lax.ppermute(x, axis, [(i, (i + by) % peers) for i in range(peers)])  13.7 us
    unnamed x23, local copies, waits for them, and re-layouts  10.9 us
    ppermute x8, starting transfers between devices, passed_along(): return lax.ppermute(x, axis, [(i, (i + by) % peers) for i in range(peers)])  10.4 us
  transfers between devices with their start and end apart: 10, of which 8 were waited for; matrix products, arithmetic and copies ran while one was open for 40% of the time, Pallas kernels for 0%

profile of v1, /device:TPU:2, one launch (start us, length us, event | category | flops | bytes accessed | tf_op | source)
XLA Modules:
  0.0 249.6 jit_solution(13117643065324391075)
XLA Ops:
  7.2 1.7 collective-permute-start
  8.9 3.9 %collective-permute-start.2 = (bf16[2,128,512]{2,1,0:T(8,128)(2,1)}, bf16[2,128,512]{2,1,0:T(8,128)(2,1)S(1)}, u32[]{:S(2)}, u32[]{:S(2)}) collective-permute-start(bf16[2,128,512]{2,1,0:T(8,128)(2,1)} %bitcast.69), channel_id=1, source_target_pairs={{0,31},{1,0},{2,1},{3,2},{4,3},{5,4},{6,5},{7,6},{8,7},{9,8},{10,9... | collective-permute-start | bytes 786440 | tf_op jit(solution)/shard_map/ppermute | solution.py:12
  14.7 2.2 fusion.33
  17.6 1.6 convert_reduce_fusion
  20.6 1.4 collective-permute-done.3
  22.0 2.8 %gather_fusion = bf16[32,128,512]{2,1,0:T(8,128)(2,1)} fusion(bf16[10,128,512]{2,1,0:T(8,128)(2,1)S(1)} %constant_dynamic-update-slice_fusion, s32[1024]{0:T(1024)S(1)} %pad_clamp_fusion), kind=kCustom, calls=%fused_computation | custom fusion | bytes 8388736 | tf_op jit(solution)/shard_map/jit(_take)/gather | solution.py:46
  24.8 3.1 %fusion.11 = bf16[2,128,512]{2,1,0:T(8,128)(2,1)S(1)} fusion(bf16[2,16,128,512]{3,2,1,0:T(8,128)(2,1)} %bitcast.66, pred[2,16]{1,0:T(4,128)(4,1)S(1)} %get-tuple-element.12, bf16[2,16,128,128]{3,2,1,0:T(8,128)(2,1)S(1)} %copy-done.1, pred[2,16]{1,0:T(4,128)(4,1)S(1)} %iota_compare_fusion, f32[2,128]{1,0:T(2,128)S(1)} %rsqrt.7), kind=kOutput, calls=%fused_computation.12 | convolution fusion | flops 539754496 | bytes 5506112 | tf_op jit(solution)/shard_map/bkij,bkjf->bif/dot_general | solution.py:49
  29.2 1.3 fusion.35
  30.5 1.3 convolution_bitcast_fusion
  32.5 1.4 fusion.14
  33.9 8.1 %copy.21 = f32[4,8,128,512]{3,1,2,0:T(8,128)} copy(f32[4,8,128,512]{3,2,1,0:T(8,128)S(1)} %bitcast.65) | data formatting | bytes 16777216
  42.0 2.2 broadcast_in_dim.35
  44.2 75.9 %scatter_fusion = f32[10,65536]{1,0:T(8,128)} fusion(f32[10,65536]{1,0:T(8,128)} %broadcast_in_dim.35, s32[32]{0:T(128)S(1)} %reshape.113, f32[32,65536]{1,0:T(8,128)} %bitcast.64), kind=kCustom, calls=%fused_computation.1 | custom fusion | flops 2097152 | bytes 25165952 | tf_op jit(solution)/shard_map/scatter-add | solution.py:74
  120.1 2.4 convert_element_type.52
  122.5 30.9 %all-reduce.5.cloned.1.call-done = (f32[512,512]{0,1:T(8,128)}, f32[512,512]{0,1:T(8,128)}) async-done(((f32[512,512]{0,1:T(8,128)}, f32[512,512]{0,1:T(8,128)}), (f32[512,512]{0,1:T(8,128)}, f32[512,512]{0,1:T(8,128)})) %all-reduce.5.cloned.1.call-update) | async-done | bytes 2097168 | tf_op jit(solution)/shard_map/psum | solution.py:64
  154.3 3.5 %collective-permute-start.4 = (bf16[2,128,512]{2,1,0:T(8,128)(2,1)S(1)}, bf16[2,128,512]{2,1,0:T(8,128)(2,1)S(1)}, u32[]{:S(2)}, u32[]{:S(2)}) collective-permute-start(bf16[2,128,512]{2,1,0:T(8,128)(2,1)S(1)} %bitcast.78), channel_id=1, source_target_pairs={{0,30},{1,31},{2,0},{3,1},{4,2},{5,3},{6,4},{7,5},{8,6},{9,7},{10,... | collective-permute-start | bytes 786440 | tf_op jit(solution)/shard_map/ppermute | solution.py:12
  158.8 4.0 %collective-permute-done.4 = bf16[2,128,512]{2,1,0:T(8,128)(2,1)S(1)} collective-permute-done((bf16[2,128,512]{2,1,0:T(8,128)(2,1)S(1)}, bf16[2,128,512]{2,1,0:T(8,128)(2,1)S(1)}, u32[]{:S(2)}, u32[]{:S(2)}) %collective-permute-start.4) | collective-permute-done | bytes 262176 | tf_op jit(solution)/shard_map/ppermute | solution.py:12
  162.8 2.8 %collective-permute-done.5 = bf16[2,128,512]{2,1,0:T(8,128)(2,1)S(1)} collective-permute-done((bf16[2,128,512]{2,1,0:T(8,128)(2,1)S(1)}, bf16[2,128,512]{2,1,0:T(8,128)(2,1)S(1)}, u32[]{:S(2)}, u32[]{:S(2)}) %collective-permute-start.5) | collective-permute-done | bytes 262176 | tf_op jit(solution)/shard_map/ppermute | solution.py:12
  165.6 1.9 collective-permute-done.6
  167.6 2.4 collective-permute-done.7
  171.1 67.2 %all-reduce.7.cloned.1.call-done = (f32[512,512]{0,1:T(8,128)}, f32[512,512]{0,1:T(8,128)}) async-done(((f32[512,512]{0,1:T(8,128)}, f32[512,512]{0,1:T(8,128)}), (f32[512,512]{0,1:T(8,128)}, f32[512,512]{0,1:T(8,128)})) %all-reduce.7.cloned.1.call-update) | async-done | bytes 2097168 | tf_op jit(solution)/shard_map/psum | solution.py:64
  238.3 1.8 broadcast_multiply_fusion
  240.2 1.3 copy.15
  241.5 1.3 copy.16
  (46 shorter events, 9.0 us)
Async XLA Ops:
  7.2 20.8 %copy-start = (bf16[512,512]{1,0:T(8,128)(2,1)S(1)}, bf16[512,512]{1,0:T(8,128)(2,1)}, u32[]{:S(2)}) copy-start(bf16[512,512]{1,0:T(8,128)(2,1)} %param.14) | copy-start | bytes 1572868
  7.2 13.3 %copy-start.2 = (bf16[256,512]{1,0:T(8,128)(2,1)S(1)}, bf16[256,512]{1,0:T(8,128)(2,1)}, u32[]{:S(2)}) copy-start(bf16[256,512]{1,0:T(8,128)(2,1)} %param.9) | copy-start | bytes 786436
  7.2 146.2 %all-reduce.5.cloned.1.call-start = ((), (), s32[]{:S(2)}) async-start(), calls=%async_computation | async-start | bytes 4194304 | tf_op jit(solution)/shard_map/psum | solution.py:64
  7.2 12.0 %collective-permute-start = (bf16[2,128,512]{2,1,0:T(8,128)(2,1)}, bf16[2,128,512]{2,1,0:T(8,128)(2,1)S(1)}, u32[]{:S(2)}, u32[]{:S(2)}) collective-permute-start(bf16[2,128,512]{2,1,0:T(8,128)(2,1)} %bitcast.67), channel_id=1, source_target_pairs={{0,2},{1,3},{2,4},{3,5},{4,6},{5,7},{6,8},{7,9},{8,10},{9,11},{10,... | collective-permute-start | bytes 786440 | tf_op jit(solution)/shard_map/ppermute | solution.py:12
  8.9 11.6 %collective-permute-start.1 = (bf16[2,128,512]{2,1,0:T(8,128)(2,1)}, bf16[2,128,512]{2,1,0:T(8,128)(2,1)S(1)}, u32[]{:S(2)}, u32[]{:S(2)}) collective-permute-start(bf16[2,128,512]{2,1,0:T(8,128)(2,1)} %bitcast.68), channel_id=1, source_target_pairs={{0,1},{1,2},{2,3},{3,4},{4,5},{5,6},{6,7},{7,8},{8,9},{9,10},{10,1... | collective-permute-start | bytes 786440 | tf_op jit(solution)/shard_map/ppermute | solution.py:12
  8.9 11.7 %collective-permute-start.2 = (bf16[2,128,512]{2,1,0:T(8,128)(2,1)}, bf16[2,128,512]{2,1,0:T(8,128)(2,1)S(1)}, u32[]{:S(2)}, u32[]{:S(2)}) collective-permute-start(bf16[2,128,512]{2,1,0:T(8,128)(2,1)} %bitcast.69), channel_id=1, source_target_pairs={{0,31},{1,0},{2,1},{3,2},{4,3},{5,4},{6,5},{7,6},{8,7},{9,8},{10,9... | collective-permute-start | bytes 786440 | tf_op jit(solution)/shard_map/ppermute | solution.py:12
  12.7 9.3 %collective-permute-start.3 = (bf16[2,128,512]{2,1,0:T(8,128)(2,1)}, bf16[2,128,512]{2,1,0:T(8,128)(2,1)S(1)}, u32[]{:S(2)}, u32[]{:S(2)}) collective-permute-start(bf16[2,128,512]{2,1,0:T(8,128)(2,1)} %bitcast.70), channel_id=1, source_target_pairs={{0,30},{1,31},{2,0},{3,1},{4,2},{5,3},{6,4},{7,5},{8,6},{9,7},{10,... | collective-permute-start | bytes 786440 | tf_op jit(solution)/shard_map/ppermute | solution.py:12
  22.0 2.8 %copy-start.1 = (bf16[2,16,128,128]{3,2,1,0:T(8,128)(2,1)S(1)}, bf16[2,16,128,128]{3,2,1,0:T(8,128)(2,1)}, u32[]{:S(2)}) copy-start(bf16[2,16,128,128]{3,2,1,0:T(8,128)(2,1)} %param.10) | copy-start | bytes 3145732
  24.8 3.1 %copy-start.4 = (f32[256,512]{1,0:T(8,128)S(1)}, f32[256,512]{1,0:T(8,128)}, u32[]{:S(2)}) copy-start(f32[256,512]{1,0:T(8,128)} %fusion.33) | copy-start | bytes 1572868
  24.8 3.1 %copy-start.5 = (bf16[256,512]{1,0:T(8,128)(2,1)S(1)}, bf16[256,512]{1,0:T(8,128)(2,1)}, u32[]{:S(2)}) copy-start(bf16[256,512]{1,0:T(8,128)(2,1)} %param.17) | copy-start | bytes 786436
  31.8 206.5 %all-reduce.7.cloned.1.call-start = ((), (), s32[]{:S(2)}) async-start(), calls=%async_computation.1 | async-start | bytes 4194304 | tf_op jit(solution)/shard_map/psum | solution.py:64
  154.2 15.9 %copy-start.3 = (bf16[512,512]{1,0:T(8,128)(2,1)S(1)}, bf16[512,512]{1,0:T(8,128)(2,1)}, u32[]{:S(2)}) copy-start(bf16[512,512]{1,0:T(8,128)(2,1)} %param.13) | copy-start | bytes 1572868
  154.3 8.6 %collective-permute-start.4 = (bf16[2,128,512]{2,1,0:T(8,128)(2,1)S(1)}, bf16[2,128,512]{2,1,0:T(8,128)(2,1)S(1)}, u32[]{:S(2)}, u32[]{:S(2)}) collective-permute-start(bf16[2,128,512]{2,1,0:T(8,128)(2,1)S(1)} %bitcast.78), channel_id=1, source_target_pairs={{0,30},{1,31},{2,0},{3,1},{4,2},{5,3},{6,4},{7,5},{8,6},{9,7},{10,... | collective-permute-start | bytes 786440 | tf_op jit(solution)/shard_map/ppermute | solution.py:12
  157.8 7.8 %collective-permute-start.5 = (bf16[2,128,512]{2,1,0:T(8,128)(2,1)S(1)}, bf16[2,128,512]{2,1,0:T(8,128)(2,1)S(1)}, u32[]{:S(2)}, u32[]{:S(2)}) collective-permute-start(bf16[2,128,512]{2,1,0:T(8,128)(2,1)S(1)} %bitcast.79), channel_id=1, source_target_pairs={{0,31},{1,0},{2,1},{3,2},{4,3},{5,4},{6,5},{7,6},{8,7},{9,8},{10,9... | collective-permute-start | bytes 786440 | tf_op jit(solution)/shard_map/ppermute | solution.py:12
  157.9 9.6 %collective-permute-start.6 = (bf16[2,128,512]{2,1,0:T(8,128)(2,1)S(1)}, bf16[2,128,512]{2,1,0:T(8,128)(2,1)S(1)}, u32[]{:S(2)}, u32[]{:S(2)}) collective-permute-start(bf16[2,128,512]{2,1,0:T(8,128)(2,1)S(1)} %bitcast.80), channel_id=1, source_target_pairs={{0,1},{1,2},{2,3},{3,4},{4,5},{5,6},{6,7},{7,8},{8,9},{9,10},{10,1... | collective-permute-start | bytes 786440 | tf_op jit(solution)/shard_map/ppermute | solution.py:12
  158.5 11.4 %collective-permute-start.7 = (bf16[2,128,512]{2,1,0:T(8,128)(2,1)S(1)}, bf16[2,128,512]{2,1,0:T(8,128)(2,1)S(1)}, u32[]{:S(2)}, u32[]{:S(2)}) collective-permute-start(bf16[2,128,512]{2,1,0:T(8,128)(2,1)S(1)} %bitcast.81), channel_id=1, source_target_pairs={{0,2},{1,3},{2,4},{3,5},{4,6},{5,7},{6,8},{7,9},{8,10},{9,11},{10,... | collective-permute-start | bytes 786440 | tf_op jit(solution)/shard_map/ppermute | solution.py:12
Sparse Core Ops, SparseCore 0:
  31.9 121.3 all-reduce.4
  155.8 82.5 all-reduce.6
